TPU v7x, 32 devices: a whole 2x2x4 slice. The times are simulated.
32 devices in a mesh: outer: 8 (over z, x), inner: 4 (over y, core).
Axes of the slice: x: 2, y: 2, z: 4, core: 2. Of those that a mesh axis runs over, the one named last changes fastest.
Arguments:
- inputs: bfloat16 [16384, 512], P(('outer', 'inner')), may hold values from -6 to 6
- weights: bfloat16 [3151872], replicated
- cotangent: bfloat16 [16384, 512], P(('outer', 'inner')), may hold values from -6 to 6
- clip_lengths: int32 [11], replicated, may hold values from 1 to 1500, 16384 in all
- first_moment: float32 [3151872], P('inner')
- second_moment: float32 [3151872], P('inner')
Outputs:
- layer_output: bfloat16 [16384, 512], P(('outer', 'inner'))
- input_grad: bfloat16 [16384, 512], P(('outer', 'inner'))
- weight_grads: float32 [3151872], P('inner')
- grad_norm: float32 [], replicated
- moment_one: float32 [3151872], P('inner')
- moment_two: float32 [3151872], P('inner')
- weight_step: bfloat16 [3151872], replicated
Inputs may be any that keep to these rules, and one draw needn't show every extreme that they name: `clip_lengths`: the lengths add up to 16384; clip c occupies the slots from the sum of the lengths before it on, in order.
All inputs are finite; a program needn't handle non-finite values.
Results may differ from a plain program's by a relative error of at most 0.015.
Values may be sent and summed in bfloat16 or wider, within the bound.
No kernel may reach another device: no remote copies, remote signals or barrier semaphores. Data moves between devices by JAX's collectives and lax.ppermute only.
A program may use at most 192 MiB of HBM per device.

v0:
```python
import math
import jax
import jax.numpy as jnp
from jax import lax
from jax.sharding import PartitionSpec as P

D = 512
HEADS = 8
FF = 2048
MOST = 1500
BETA_ONE = 0.9
BETA_TWO = 0.999
FIX_ONE = 1.0 - (0.9**10) ** 10
FIX_TWO = 1.0 - (0.999**10) ** 10
DECAY = 0.1
INV_ROOT_TWO = 1.0 / math.sqrt(2.0)
INV_ROOT_TWO_PI = 1.0 / math.sqrt(2.0 * math.pi)


def passed_along(block, axis, distance):
    devices = range(lax.axis_size(axis))
    route = [(i - distance, i) for i in devices if i - distance in devices]
    return lax.ppermute(block, axis, route)


def layouts():
    return [
        (D,),
        (D,),
        (D, D),
        (D,),
        (D, D),
        (D, D),
        (D,),
        (D, D),
        (D,),
        (D,),
        (D,),
        (D, FF),
        (FF,),
        (FF, D),
        (D,),
    ]


def unpack(flat):
    sections = []
    offset = 0
    for layout in layouts():
        entries = 1
        for extent in layout:
            entries = entries * extent
        section = flat[offset : offset + entries].reshape(layout)
        if len(layout) == 1:
            section = section.astype(jnp.float32)
        sections.append(section)
        offset = offset + entries
    return sections


def plain_dot(matrix_one, matrix_two):
    return jnp.dot(matrix_one, matrix_two, preferred_element_type=jnp.float32)


def rows_dot(matrix_one, matrix_two):
    return lax.dot_general(
        matrix_one, matrix_two, (((0,), (0,)), ((), ())), preferred_element_type=jnp.float32
    )


def back_dot(matrix_one, matrix_two):
    return lax.dot_general(
        matrix_one, matrix_two, (((1,), (1,)), ((), ())), preferred_element_type=jnp.float32
    )


def standard(values):
    center = jnp.mean(values, axis=-1, keepdims=True)
    centered = values - center
    inverse_dev = lax.rsqrt(jnp.mean(centered * centered, axis=-1, keepdims=True) + 1e-05)
    return (centered * inverse_dev, inverse_dev)


def norm_back(grad_normed, normed_hat, inverse_dev, gain):
    scaled = grad_normed * gain
    return inverse_dev * (
        scaled
        - jnp.mean(scaled, axis=-1, keepdims=True)
        - normed_hat * jnp.mean(scaled * normed_hat, axis=-1, keepdims=True)
    )


def bounds(positions, clip_lengths):
    starts = jnp.cumsum(clip_lengths, dtype=jnp.int32) - clip_lengths
    member = (
        jnp.sum((positions[:, None] >= starts[None, :]).astype(jnp.int32), axis=1, dtype=jnp.int32)
        - 1
    )
    onehot = (
        jnp.arange(clip_lengths.shape[0], dtype=jnp.int32)[None, :] == member[:, None]
    ).astype(jnp.int32)
    lower_slot = jnp.sum(onehot * starts[None, :], axis=1, dtype=jnp.int32)
    upper_slot = lower_slot + jnp.sum(onehot * clip_lengths[None, :], axis=1, dtype=jnp.int32)
    return (lower_slot, upper_slot)


def fetch_keys(pair, distance):
    return passed_along((pair[0], pair[1]), ("outer", "inner"), -distance)


def return_grads(pair, distance):
    return (
        passed_along(pair[0].astype(jnp.bfloat16), ("outer", "inner"), distance).astype(
            jnp.float32
        ),
        passed_along(pair[1].astype(jnp.bfloat16), ("outer", "inner"), distance).astype(
            jnp.float32
        ),
    )


def on_device(inputs, weights, cotangent, clip_lengths, first_moment, second_moment):
    tok_rows = inputs.shape[0]
    reach = (MOST + tok_rows - 2) // tok_rows
    head_width = D // HEADS
    score_scale = 1.0 / math.sqrt(head_width)
    (
        first_gain,
        first_bias,
        query_weight,
        query_bias,
        key_weight,
        value_weight,
        value_bias,
        out_weight,
        out_bias,
        second_gain,
        second_bias,
        up_weight,
        up_bias,
        down_weight,
        down_bias,
    ) = unpack(weights)
    base_slot = lax.axis_index(("outer", "inner")) * tok_rows
    positions = base_slot + jnp.arange(tok_rows, dtype=jnp.int32)
    lower_slot, upper_slot = bounds(positions, clip_lengths)
    input_rows = inputs.astype(jnp.float32)
    first_hat, first_dev = standard(input_rows)
    normed = (first_hat * first_gain + first_bias).astype(jnp.bfloat16)
    query_rows = (plain_dot(normed, query_weight) + query_bias).astype(jnp.bfloat16)
    key_rows = plain_dot(normed, key_weight).astype(jnp.bfloat16)
    value_rows = (plain_dot(normed, value_weight) + value_bias).astype(jnp.bfloat16)
    distances = list(range(-reach, reach + 1))
    key_list = []
    value_list = []
    for distance in distances:
        if distance == 0:
            pair = (key_rows, value_rows)
        else:
            pair = fetch_keys((key_rows, value_rows), distance)
        key_list.append(pair[0])
        value_list.append(pair[1])
    block_count = len(distances)
    key_stack = jnp.stack(key_list).reshape(block_count, tok_rows, HEADS, head_width)
    value_stack = jnp.stack(value_list).reshape(block_count, tok_rows, HEADS, head_width)
    block_shift = jnp.arange(-reach, reach + 1, dtype=jnp.int32)
    query_heads = query_rows.reshape(tok_rows, HEADS, head_width)

    def block_scores(key_block, shift_block):
        places = base_slot + shift_block * tok_rows + jnp.arange(tok_rows, dtype=jnp.int32)
        allowed = (places[None, :] >= lower_slot[:, None]) & (places[None, :] < upper_slot[:, None])
        raw_scores = jnp.einsum(
            "qhd,khd->hqk", query_heads, key_block, preferred_element_type=jnp.float32
        )
        return jnp.where(allowed[None], score_scale * raw_scores, -1e30)

    def first_pass(carried, block_data):
        row_peak, row_total = carried
        key_block, shift_block = block_data
        scores = block_scores(key_block, shift_block)
        new_peak = jnp.maximum(row_peak, jnp.max(scores, axis=-1))
        row_total = row_total * jnp.exp(row_peak - new_peak) + jnp.sum(
            jnp.exp(scores - new_peak[:, :, None]), axis=-1
        )
        return ((new_peak, row_total), None)

    start_peak = jnp.full((HEADS, tok_rows), -1e30, jnp.float32)
    start_total = jnp.zeros((HEADS, tok_rows), jnp.float32)
    (row_peak, row_total), _ = lax.scan(
        first_pass, (start_peak, start_total), (key_stack, block_shift)
    )
    log_total = row_peak + jnp.log(row_total)

    def second_pass(carried, block_data):
        key_block, value_block, shift_block = block_data
        soft_weights = jnp.exp(block_scores(key_block, shift_block) - log_total[:, :, None])
        return (
            carried
            + jnp.einsum(
                "hqk,khd->qhd",
                soft_weights.astype(jnp.bfloat16),
                value_block,
                preferred_element_type=jnp.float32,
            ),
            None,
        )

    attended, _ = lax.scan(
        second_pass,
        jnp.zeros((tok_rows, HEADS, head_width), jnp.float32),
        (key_stack, value_stack, block_shift),
    )
    mixed = attended.reshape(tok_rows, D).astype(jnp.bfloat16)
    middle = input_rows + plain_dot(mixed, out_weight) + out_bias
    second_hat, second_dev = standard(middle)
    hidden_in = (second_hat * second_gain + second_bias).astype(jnp.bfloat16)
    up_rows = plain_dot(hidden_in, up_weight) + up_bias
    cdf_part = 0.5 * (1.0 + lax.erf(up_rows * INV_ROOT_TWO))
    activated = (up_rows * cdf_part).astype(jnp.bfloat16)
    layer_output = (middle + plain_dot(activated, down_weight) + down_bias).astype(jnp.bfloat16)
    grad_out = cotangent.astype(jnp.float32)
    down_grad = rows_dot(activated, cotangent)
    down_bias_grad = jnp.sum(grad_out, axis=0)
    grad_act = back_dot(cotangent, down_weight)
    pdf_part = jnp.exp(-0.5 * up_rows * up_rows) * INV_ROOT_TWO_PI
    grad_up = (grad_act * (cdf_part + up_rows * pdf_part)).astype(jnp.bfloat16)
    up_grad = rows_dot(hidden_in, grad_up)
    up_bias_grad = jnp.sum(grad_up.astype(jnp.float32), axis=0)
    grad_hidden = back_dot(grad_up, up_weight)
    second_gain_grad = jnp.sum(grad_hidden * second_hat, axis=0)
    second_bias_grad = jnp.sum(grad_hidden, axis=0)
    grad_middle = grad_out + norm_back(grad_hidden, second_hat, second_dev, second_gain)
    grad_branch = grad_middle.astype(jnp.bfloat16)
    out_grad = rows_dot(mixed, grad_branch)
    out_bias_grad = jnp.sum(grad_branch.astype(jnp.float32), axis=0)
    grad_mixed = back_dot(grad_branch, out_weight).astype(jnp.bfloat16)
    grad_heads = grad_mixed.reshape(tok_rows, HEADS, head_width)
    row_delta = jnp.sum(grad_heads.astype(jnp.float32) * attended, axis=-1).T

    def back_pass(grad_query, block_data):
        key_block, value_block, shift_block = block_data
        soft_weights = jnp.exp(block_scores(key_block, shift_block) - log_total[:, :, None])
        grad_probs = jnp.einsum(
            "qhd,khd->hqk", grad_heads, value_block, preferred_element_type=jnp.float32
        )
        grad_scores = (score_scale * soft_weights * (grad_probs - row_delta[:, :, None])).astype(
            jnp.bfloat16
        )
        value_part = jnp.einsum(
            "hqk,qhd->khd",
            soft_weights.astype(jnp.bfloat16),
            grad_heads,
            preferred_element_type=jnp.float32,
        )
        key_part = jnp.einsum(
            "hqk,qhd->khd", grad_scores, query_heads, preferred_element_type=jnp.float32
        )
        grad_query = grad_query + jnp.einsum(
            "hqk,khd->qhd", grad_scores, key_block, preferred_element_type=jnp.float32
        )
        return (grad_query, (key_part, value_part))

    grad_query, (key_parts, value_parts) = lax.scan(
        back_pass,
        jnp.zeros((tok_rows, HEADS, head_width), jnp.float32),
        (key_stack, value_stack, block_shift),
    )
    grad_keys = key_parts[reach]
    grad_values = value_parts[reach]
    for position, distance in enumerate(distances):
        if distance != 0:
            got_pair = return_grads((key_parts[position], value_parts[position]), distance)
            grad_keys = grad_keys + got_pair[0]
            grad_values = grad_values + got_pair[1]
    query_low = grad_query.reshape(tok_rows, D).astype(jnp.bfloat16)
    key_low = grad_keys.reshape(tok_rows, D).astype(jnp.bfloat16)
    value_low = grad_values.reshape(tok_rows, D).astype(jnp.bfloat16)
    query_grad = rows_dot(normed, query_low)
    query_bias_grad = jnp.sum(query_low.astype(jnp.float32), axis=0)
    key_grad = rows_dot(normed, key_low)
    value_grad = rows_dot(normed, value_low)
    value_bias_grad = jnp.sum(value_low.astype(jnp.float32), axis=0)
    grad_normed = (
        back_dot(query_low, query_weight)
        + back_dot(key_low, key_weight)
        + back_dot(value_low, value_weight)
    )
    first_gain_grad = jnp.sum(grad_normed * first_hat, axis=0)
    first_bias_grad = jnp.sum(grad_normed, axis=0)
    input_grad = (grad_middle + norm_back(grad_normed, first_hat, first_dev, first_gain)).astype(
        jnp.bfloat16
    )
    packed = jnp.concatenate(
        [
            section.reshape(-1)
            for section in [
                first_gain_grad,
                first_bias_grad,
                query_grad,
                query_bias_grad,
                key_grad,
                value_grad,
                value_bias_grad,
                out_grad,
                out_bias_grad,
                second_gain_grad,
                second_bias_grad,
                up_grad,
                up_bias_grad,
                down_grad,
                down_bias_grad,
            ]
        ]
    )
    group_shard = lax.psum_scatter(
        packed.astype(jnp.bfloat16), "inner", scatter_dimension=0, tiled=True
    )
    grad_shard = lax.psum(group_shard, "outer").astype(jnp.float32)
    squares = lax.psum(jnp.sum(grad_shard * grad_shard), "inner")
    grad_norm = jnp.sqrt(squares)
    clipped = grad_shard / jnp.maximum(grad_norm, 1.0)
    moment_one = BETA_ONE * first_moment + (1.0 - BETA_ONE) * clipped
    moment_two = BETA_TWO * second_moment + (1.0 - BETA_TWO) * clipped * clipped
    shard_len = grad_shard.shape[0]
    own_weights = lax.dynamic_slice_in_dim(
        weights, lax.axis_index("inner") * shard_len, shard_len, 0
    ).astype(jnp.float32)
    update = moment_one / FIX_ONE / (jnp.sqrt(moment_two / FIX_TWO) + 1e-08) + DECAY * own_weights
    step_piece = update.astype(jnp.bfloat16)
    weight_step = lax.all_gather(step_piece, "inner", axis=0, tiled=True)
    return (layer_output, input_grad, grad_shard, grad_norm, moment_one, moment_two, weight_step)


def solution(mesh):
    return jax.shard_map(
        on_device,
        mesh=mesh,
        in_specs=(
            P(("outer", "inner"), None),
            P(),
            P(("outer", "inner"), None),
            P(),
            P("inner"),
            P("inner"),
        ),
        out_specs=(
            P(("outer", "inner"), None),
            P(("outer", "inner"), None),
            P("inner"),
            P(),
            P("inner"),
            P("inner"),
            P(),
        ),
        check_vma=False,
    )
```

profile of v0, /device:TPU:0, one launch (start us, length us, event | category | flops | bytes accessed | tf_op | source)
XLA Modules:
  0.0 1054.3 jit_solution(2918028599666637666)
XLA Ops:
  27.7 5.2 fusion.115
  49.2 7.0 collective-permute-done.7
  59.4 11.3 %collective-permute-start.1 = (bf16[512,512]{0,1:T(8,128)(2,1)}, bf16[512,512]{0,1:T(8,128)(2,1)}, u32[]{:S(2)}, u32[]{:S(2)}) collective-permute-start(bf16[512,512]{0,1:T(8,128)(2,1)} %fusion.69), channel_id=1, source_target_pairs={{0,2},{1,3},{2,4},{3,5},{4,6},{5,7},{6,8},{7,9},{8,10},{9,11},{10,... | collective-permute-start | bytes 1572872 | tf_op jit(solution)/shard_map/ppermute | solution.py:23
  81.6 87.1 %while.39 = (s32[]{:T(128)}, f32[8,512]{1,0:T(8,128)S(1)}, f32[8,512]{1,0:T(8,128)S(1)}, s32[7]{0:T(128)S(1)}, s32[]{:T(128)}, /*index=5*/s32[512]{0:T(512)S(1)}...) while((s32[]{:T(128)}, f32[8,512]{1,0:T(8,128)S(1)}, ...), condition=%wide.region_9.10_spmd.clone, body=%wide.region_6.9_spmd.clone.sunk | while | flops 283922944 | bytes 18833588 | solution.py:189
  83.1 5.8 fusion.179
  95.6 5.8 fusion.179
  108.0 5.8 fusion.179
  120.5 5.8 fusion.179
  132.9 5.8 fusion.179
  145.4 5.8 fusion.179
  157.8 5.8 fusion.179
  182.7 47.9 %while.40 = (s32[]{:T(128)}, f32[512,8,64]{0,2,1:T(8,128)}, bf16[7,512,8,64]{1,3,2,0:T(8,128)(2,1)}, s32[7]{0:T(128)S(1)}, s32[]{:T(128)}, /*index=5*/s32[512]{0...) while((s32[]{:T(128)}, f32[512,8,64]{0,2,1:T(8,128)}, ...), condition=%wide.region_11.12_spmd.clone, body=%wide.region_10.11_spmd.clone.sunk | while | flops 546570752 | bytes 4220598 | solution.py:208
  190.8 5.4 fusion.185
  197.7 5.4 fusion.185
  204.6 5.4 fusion.185
  211.5 5.4 fusion.185
  218.4 5.4 fusion.185
  225.3 5.4 fusion.185
  251.3 183.3 %while.41 = (s32[]{:T(128)}, f32[512,8,64]{0,2,1:T(8,128)S(1)}, f32[7,512,8,64]{1,3,2,0:T(8,128)}, f32[7,512,8,64]{1,3,2,0:T(8,128)}, bf16[7,512,8,64]{1,3,2,0:T...) while((s32[]{:T(128)}, f32[512,8,64]{0,2,1:T(8,128)S(1)}, ...), condition=%wide.region_18.19_spmd.clone, body=%wide.region_17.18_spmd.clone.sunk | while | flops 1366557184 | bytes 96788768 | solution.py:263
  251.5 5.6 fusion.196
  258.6 8.6 fusion.197
  277.6 5.6 fusion.196
  284.7 8.6 fusion.197
  303.8 5.6 fusion.196
  310.9 8.6 fusion.197
  330.0 5.6 fusion.196
  337.1 8.6 fusion.197
  356.1 5.6 fusion.196
  363.2 8.6 fusion.197
  382.3 5.6 fusion.196
  389.4 8.6 fusion.197
  408.4 5.6 fusion.196
  415.5 8.6 fusion.197
  440.0 20.0 %collective-permute-start.23 = (bf16[512,8,64]{0,2,1:T(8,128)(2,1)}, bf16[512,8,64]{0,2,1:T(8,128)(2,1)}, u32[]{:S(2)}, u32[]{:S(2)}) collective-permute-start(bf16[512,8,64]{0,2,1:T(8,128)(2,1)} %get-tuple-element.446), channel_id=1, source_target_pairs={{0,3},{1,4},{2,5},{3,6},{4,7},{5,8},{6,9},{7,10},{8,11},{9,12},{10... | collective-permute-start | bytes 1572872 | tf_op jit(solution)/shard_map/ppermute | solution.py:23
  460.0 9.7 collective-permute-start.22
  481.6 22.4 %collective-permute-done.22 = bf16[512,8,64]{0,2,1:T(8,128)(2,1)} collective-permute-done((bf16[512,8,64]{0,2,1:T(8,128)(2,1)}, bf16[512,8,64]{0,2,1:T(8,128)(2,1)}, u32[]{:S(2)}, u32[]{:S(2)}) %collective-permute-start.22) | collective-permute-done | bytes 524320 | tf_op jit(solution)/shard_map/ppermute | solution.py:23
  529.3 18.1 %collective-permute-done.13 = bf16[512,8,64]{0,2,1:T(8,128)(2,1)S(1)} collective-permute-done((bf16[512,8,64]{0,2,1:T(8,128)(2,1)S(1)}, bf16[512,8,64]{0,2,1:T(8,128)(2,1)S(1)}, u32[]{:S(2)}, u32[]{:S(2)}) %collective-permute-start.13) | collective-permute-done | bytes 524320 | tf_op jit(solution)/shard_map/ppermute | solution.py:23
  564.2 9.1 dynamic-update-slice.4
  573.2 9.1 dynamic-update-slice.5
  588.8 33.0 %dynamic-update-slice.11 = bf16[3151872]{0:T(1024)(128)(2,1)} dynamic-update-slice(bf16[3151872]{0:T(1024)(128)(2,1)} %dynamic-update-slice.10, bf16[1048576]{0:T(1024)(128)(2,1)} %bitcast.268, s32[]{} %constant.145) | dynamic-update-slice | bytes 4194308
  623.3 32.9 %dynamic-update-slice.13 = bf16[3151872]{0:T(1024)(128)(2,1)} dynamic-update-slice(bf16[3151872]{0:T(1024)(128)(2,1)} %dynamic-update-slice.12, bf16[1048576]{0:T(1024)(128)(2,1)} %bitcast.267, s32[]{} %constant.147) | dynamic-update-slice | bytes 4194308
  658.9 139.7 %all-reduce.6.cloned.1.call-done = bf16[3151872]{0:T(1024)(128)(2,1)} async-done(((bf16[3151872]{0:T(1024)(128)(2,1)}), bf16[3151872]{0:T(1024)(128)(2,1)}) %all-reduce.6.cloned.1.call-update) | async-done | bytes 6303760
  802.1 91.0 %all-reduce.4.cloned.1.call-done = bf16[787968]{0:T(1024)(128)(2,1)} async-done(((bf16[787968]{0:T(1024)(128)(2,1)}), bf16[787968]{0:T(1024)(128)(2,1)}) %all-reduce.4.cloned.1.call-update) | async-done | bytes 1575952 | tf_op jit(solution)/shard_map/psum | solution.py:318
  897.5 7.6 psum.15
  905.8 7.4 add_convert_fusion
  923.8 73.4 %all-gather.3.cloned.1.call-done = bf16[4,1,787968]{2,1,0:T(2,128)(2,1)} async-done(((bf16[1,1,787968]{2,1,0:T(2,128)(2,1)}), bf16[4,1,787968]{2,1,0:T(2,128)(2,1)}) %all-gather.3.cloned.1.call-update) | async-done | bytes 6303760 | tf_op jit(solution)/shard_map/all_gather | solution.py:330
  997.1 41.4 %reduce.7 = bf16[4,787968]{1,0:T(4,128)(2,1)} reduce(bf16[4,1,787968]{2,1,0:T(2,128)(2,1)} %all-gather.3.cloned.1.call-done, bf16[]{:T(256)} %constant.133), dimensions={1}, to_apply=%all-gather.reduce_sub_computation | reduce | bytes 12607490 | tf_op jit(solution)/shard_map/all_gather | solution.py:330
  1038.5 7.9 reshape.423
  (372 shorter events, 304.3 us)
Async XLA Ops:
  7.2 791.4 %all-reduce.6.cloned.1.call-start = ((), (), s32[]{:S(2)}) async-start(), calls=%async_computation.2 | async-start | bytes 12607488
  8.7 26.5 %copy-start.28 = (f32[512]{0:T(512)}, f32[512]{0:T(512)S(1)}, u32[]{:S(2)}) copy-start(f32[512]{0:T(512)S(1)} %get-tuple-element.438) | copy-start | bytes 6148
  8.7 26.5 %copy-start.33 = (f32[512]{0:T(512)}, f32[512]{0:T(512)S(1)}, u32[]{:S(2)}) copy-start(f32[512]{0:T(512)S(1)} %get-tuple-element.437) | copy-start | bytes 6148
  10.8 24.4 %copy-start.26 = (f32[512]{0:T(512)}, f32[512]{0:T(512)S(1)}, u32[]{:S(2)}) copy-start(f32[512]{0:T(512)S(1)} %broadcast_multiply_fusion.5) | copy-start | bytes 6148
  11.0 24.2 %copy-start.30 = (f32[512]{0:T(512)}, f32[512]{0:T(512)S(1)}, u32[]{:S(2)}) copy-start(f32[512]{0:T(512)S(1)} %add_rsqrt_fusion.1) | copy-start | bytes 6148
  11.3 21.6 %copy-start.16 = (bf16[512,512]{1,0:T(8,128)(2,1)}, bf16[512,512]{1,0:T(8,128)(2,1)S(1)}, u32[]{:S(2)}) copy-start(bf16[512,512]{1,0:T(8,128)(2,1)S(1)} %slice.155) | copy-start | bytes 1572868
  12.8 34.1 %collective-permute-start.6 = (bf16[512,512]{0,1:T(8,128)(2,1)}, bf16[512,512]{0,1:T(8,128)(2,1)}, u32[]{:S(2)}, u32[]{:S(2)}) collective-permute-start(bf16[512,512]{0,1:T(8,128)(2,1)} %convolution_convert_fusion.7), channel_id=1, source_target_pairs={{0,3},{1,4},{2,5},{3,6},{4,7},{5,8},{6,9},{7,10},{8,11},{9,12},{10... | collective-permute-start | bytes 1572872 | tf_op jit(solution)/shard_map/ppermute | solution.py:23
  17.9 38.3 %collective-permute-start.7 = (bf16[512,512]{0,1:T(8,128)(2,1)}, bf16[512,512]{0,1:T(8,128)(2,1)}, u32[]{:S(2)}, u32[]{:S(2)}) collective-permute-start(bf16[512,512]{0,1:T(8,128)(2,1)} %convolution_convert_fusion.7), channel_id=1, source_target_pairs={{0,2},{1,3},{2,4},{3,5},{4,6},{5,7},{6,8},{7,9},{8,10},{9,11},{10,... | collective-permute-start | bytes 1572872 | tf_op jit(solution)/shard_map/ppermute | solution.py:23
  22.1 37.3 %collective-permute-start.8 = (bf16[512,512]{0,1:T(8,128)(2,1)}, bf16[512,512]{0,1:T(8,128)(2,1)}, u32[]{:S(2)}, u32[]{:S(2)}) collective-permute-start(bf16[512,512]{0,1:T(8,128)(2,1)} %convolution_convert_fusion.7), channel_id=1, source_target_pairs={{0,1},{1,2},{2,3},{3,4},{4,5},{5,6},{6,7},{7,8},{8,9},{9,10},{10,1... | collective-permute-start | bytes 1572872 | tf_op jit(solution)/shard_map/ppermute | solution.py:23
  24.4 48.4 %collective-permute-start.9 = (bf16[512,512]{0,1:T(8,128)(2,1)}, bf16[512,512]{0,1:T(8,128)(2,1)}, u32[]{:S(2)}, u32[]{:S(2)}) collective-permute-start(bf16[512,512]{0,1:T(8,128)(2,1)} %convolution_convert_fusion.7), channel_id=1, source_target_pairs={{1,0},{2,1},{3,2},{4,3},{5,4},{6,5},{7,6},{8,7},{9,8},{10,9},{11,1... | collective-permute-start | bytes 1572872 | tf_op jit(solution)/shard_map/ppermute | solution.py:23
  25.7 50.3 %collective-permute-start.10 = (bf16[512,512]{0,1:T(8,128)(2,1)}, bf16[512,512]{0,1:T(8,128)(2,1)}, u32[]{:S(2)}, u32[]{:S(2)}) collective-permute-start(bf16[512,512]{0,1:T(8,128)(2,1)} %convolution_convert_fusion.7), channel_id=1, source_target_pairs={{2,0},{3,1},{4,2},{5,3},{6,4},{7,5},{8,6},{9,7},{10,8},{11,9},{12,... | collective-permute-start | bytes 1572872 | tf_op jit(solution)/shard_map/ppermute | solution.py:23
  37.2 8.6 copy-start.12
  46.8 31.6 %collective-permute-start.11 = (bf16[512,512]{0,1:T(8,128)(2,1)}, bf16[512,512]{0,1:T(8,128)(2,1)S(1)}, u32[]{:S(2)}, u32[]{:S(2)}) collective-permute-start(bf16[512,512]{0,1:T(8,128)(2,1)} %convolution_convert_fusion.7), channel_id=1, source_target_pairs={{3,0},{4,1},{5,2},{6,3},{7,4},{8,5},{9,6},{10,7},{11,8},{12,9},{13... | collective-permute-start | bytes 1572872 | tf_op jit(solution)/shard_map/ppermute | solution.py:23
  56.2 112.5 %collective-permute-start = (bf16[512,512]{0,1:T(8,128)(2,1)}, bf16[512,512]{0,1:T(8,128)(2,1)}, u32[]{:S(2)}, u32[]{:S(2)}) collective-permute-start(bf16[512,512]{0,1:T(8,128)(2,1)} %fusion.69), channel_id=1, source_target_pairs={{0,3},{1,4},{2,5},{3,6},{4,7},{5,8},{6,9},{7,10},{8,11},{9,12},{10... | collective-permute-start | bytes 1572872 | tf_op jit(solution)/shard_map/ppermute | solution.py:23
  59.4 111.9 %collective-permute-start.1 = (bf16[512,512]{0,1:T(8,128)(2,1)}, bf16[512,512]{0,1:T(8,128)(2,1)}, u32[]{:S(2)}, u32[]{:S(2)}) collective-permute-start(bf16[512,512]{0,1:T(8,128)(2,1)} %fusion.69), channel_id=1, source_target_pairs={{0,2},{1,3},{2,4},{3,5},{4,6},{5,7},{6,8},{7,9},{8,10},{9,11},{10,... | collective-permute-start | bytes 1572872 | tf_op jit(solution)/shard_map/ppermute | solution.py:23
  72.8 99.6 %collective-permute-start.2 = (bf16[512,512]{0,1:T(8,128)(2,1)}, bf16[512,512]{0,1:T(8,128)(2,1)}, u32[]{:S(2)}, u32[]{:S(2)}) collective-permute-start(bf16[512,512]{0,1:T(8,128)(2,1)} %fusion.69), channel_id=1, source_target_pairs={{0,1},{1,2},{2,3},{3,4},{4,5},{5,6},{6,7},{7,8},{8,9},{9,10},{10,1... | collective-permute-start | bytes 1572872 | tf_op jit(solution)/shard_map/ppermute | solution.py:23
  76.0 98.5 %collective-permute-start.3 = (bf16[512,512]{0,1:T(8,128)(2,1)}, bf16[512,512]{0,1:T(8,128)(2,1)}, u32[]{:S(2)}, u32[]{:S(2)}) collective-permute-start(bf16[512,512]{0,1:T(8,128)(2,1)} %fusion.69), channel_id=1, source_target_pairs={{1,0},{2,1},{3,2},{4,3},{5,4},{6,5},{7,6},{8,7},{9,8},{10,9},{11,1... | collective-permute-start | bytes 1572872 | tf_op jit(solution)/shard_map/ppermute | solution.py:23
  78.4 97.2 %collective-permute-start.4 = (bf16[512,512]{0,1:T(8,128)(2,1)}, bf16[512,512]{0,1:T(8,128)(2,1)}, u32[]{:S(2)}, u32[]{:S(2)}) collective-permute-start(bf16[512,512]{0,1:T(8,128)(2,1)} %fusion.69), channel_id=1, source_target_pairs={{2,0},{3,1},{4,2},{5,3},{6,4},{7,5},{8,6},{9,7},{10,8},{11,9},{12,... | collective-permute-start | bytes 1572872 | tf_op jit(solution)/shard_map/ppermute | solution.py:23
  168.7 12.1 %collective-permute-start.5 = (bf16[512,512]{0,1:T(8,128)(2,1)}, bf16[512,512]{0,1:T(8,128)(2,1)S(1)}, u32[]{:S(2)}, u32[]{:S(2)}) collective-permute-start(bf16[512,512]{0,1:T(8,128)(2,1)} %fusion.69), channel_id=1, source_target_pairs={{3,0},{4,1},{5,2},{6,3},{7,4},{8,5},{9,6},{10,7},{11,8},{12,9},{13... | collective-permute-start | bytes 1572872 | tf_op jit(solution)/shard_map/ppermute | solution.py:23
  267.2 6.2 copy-start.1
  293.4 6.2 copy-start.1
  319.5 6.2 copy-start.1
  345.7 6.2 copy-start.1
  371.9 6.2 copy-start.1
  398.0 6.2 copy-start.1
  424.2 6.2 copy-start.1
  438.2 31.4 %copy-start.14 = (bf16[512,512]{1,0:T(8,128)(2,1)S(1)}, bf16[512,512]{1,0:T(8,128)(2,1)}, u32[]{:S(2)}) copy-start(bf16[512,512]{1,0:T(8,128)(2,1)} %param.14) | copy-start | bytes 1572868
  440.0 40.3 %collective-permute-start.23 = (bf16[512,8,64]{0,2,1:T(8,128)(2,1)}, bf16[512,8,64]{0,2,1:T(8,128)(2,1)}, u32[]{:S(2)}, u32[]{:S(2)}) collective-permute-start(bf16[512,8,64]{0,2,1:T(8,128)(2,1)} %get-tuple-element.446), channel_id=1, source_target_pairs={{0,3},{1,4},{2,5},{3,6},{4,7},{5,8},{6,9},{7,10},{8,11},{9,12},{10... | collective-permute-start | bytes 1572872 | tf_op jit(solution)/shard_map/ppermute | solution.py:23
  460.0 44.0 %collective-permute-start.22 = (bf16[512,8,64]{0,2,1:T(8,128)(2,1)}, bf16[512,8,64]{0,2,1:T(8,128)(2,1)}, u32[]{:S(2)}, u32[]{:S(2)}) collective-permute-start(bf16[512,8,64]{0,2,1:T(8,128)(2,1)} %get-tuple-element.447), channel_id=1, source_target_pairs={{0,2},{1,3},{2,4},{3,5},{4,6},{5,7},{6,8},{7,9},{8,10},{9,11},{10,... | collective-permute-start | bytes 1572872 | tf_op jit(solution)/shard_map/ppermute | solution.py:23
  469.8 45.2 %collective-permute-start.21 = (bf16[512,8,64]{0,2,1:T(8,128)(2,1)}, bf16[512,8,64]{0,2,1:T(8,128)(2,1)S(1)}, u32[]{:S(2)}, u32[]{:S(2)}) collective-permute-start(bf16[512,8,64]{0,2,1:T(8,128)(2,1)} %get-tuple-element.448), channel_id=1, source_target_pairs={{0,1},{1,2},{2,3},{3,4},{4,5},{5,6},{6,7},{7,8},{8,9},{9,10},{10,1... | collective-permute-start | bytes 1572872 | tf_op jit(solution)/shard_map/ppermute | solution.py:23
  472.1 45.1 %collective-permute-start.20 = (bf16[512,8,64]{0,2,1:T(8,128)(2,1)}, bf16[512,8,64]{0,2,1:T(8,128)(2,1)S(1)}, u32[]{:S(2)}, u32[]{:S(2)}) collective-permute-start(bf16[512,8,64]{0,2,1:T(8,128)(2,1)} %get-tuple-element.449), channel_id=1, source_target_pairs={{1,0},{2,1},{3,2},{4,3},{5,4},{6,5},{7,6},{8,7},{9,8},{10,9},{11,1... | collective-permute-start | bytes 1572872 | tf_op jit(solution)/shard_map/ppermute | solution.py:23
  473.4 46.5 %collective-permute-start.19 = (bf16[512,8,64]{0,2,1:T(8,128)(2,1)}, bf16[512,8,64]{0,2,1:T(8,128)(2,1)S(1)}, u32[]{:S(2)}, u32[]{:S(2)}) collective-permute-start(bf16[512,8,64]{0,2,1:T(8,128)(2,1)} %get-tuple-element.450), channel_id=1, source_target_pairs={{2,0},{3,1},{4,2},{5,3},{6,4},{7,5},{8,6},{9,7},{10,8},{11,9},{12,... | collective-permute-start | bytes 1572872 | tf_op jit(solution)/shard_map/ppermute | solution.py:23
  479.0 28.9 %copy-start.39 = (bf16[512,2048]{1,0:T(8,128)(2,1)S(1)}, bf16[512,2048]{1,0:T(8,128)(2,1)}, u32[]{:S(2)}) copy-start(bf16[512,2048]{1,0:T(8,128)(2,1)} %copy-done.38) | copy-start | bytes 6291460
  480.3 40.9 %collective-permute-start.18 = (bf16[512,8,64]{0,2,1:T(8,128)(2,1)S(1)}, bf16[512,8,64]{0,2,1:T(8,128)(2,1)S(1)}, u32[]{:S(2)}, u32[]{:S(2)}) collective-permute-start(bf16[512,8,64]{0,2,1:T(8,128)(2,1)S(1)} %copy-done.20), channel_id=1, source_target_pairs={{3,0},{4,1},{5,2},{6,3},{7,4},{8,5},{9,6},{10,7},{11,8},{12,9},{13... | collective-permute-start | bytes 1572872 | tf_op jit(solution)/shard_map/ppermute | solution.py:23
  504.0 18.6 %collective-permute-start.17 = (bf16[512,8,64]{0,2,1:T(8,128)(2,1)S(1)}, bf16[512,8,64]{0,2,1:T(8,128)(2,1)S(1)}, u32[]{:S(2)}, u32[]{:S(2)}) collective-permute-start(bf16[512,8,64]{0,2,1:T(8,128)(2,1)S(1)} %get-tuple-element.452), channel_id=1, source_target_pairs={{0,3},{1,4},{2,5},{3,6},{4,7},{5,8},{6,9},{7,10},{8,11},{9,12},{10... | collective-permute-start | bytes 1572872 | tf_op jit(solution)/shard_map/ppermute | solution.py:23
  514.9 11.1 %copy-start.27 = (f32[512]{0:T(512)S(1)}, f32[512]{0:T(512)}, u32[]{:S(2)}) copy-start(f32[512]{0:T(512)} %copy-done.26) | copy-start | bytes 6148
  514.9 11.1 %copy-start.29 = (f32[512]{0:T(512)S(1)}, f32[512]{0:T(512)}, u32[]{:S(2)}) copy-start(f32[512]{0:T(512)} %copy-done.28) | copy-start | bytes 6148
  515.0 11.1 %copy-start.31 = (f32[512]{0:T(512)S(1)}, f32[512]{0:T(512)}, u32[]{:S(2)}) copy-start(f32[512]{0:T(512)} %copy-done.30) | copy-start | bytes 6148
  515.0 11.1 %copy-start.34 = (f32[512]{0:T(512)S(1)}, f32[512]{0:T(512)}, u32[]{:S(2)}) copy-start(f32[512]{0:T(512)} %copy-done.33) | copy-start | bytes 6148
  515.0 14.4 %collective-permute-start.16 = (bf16[512,8,64]{0,2,1:T(8,128)(2,1)S(1)}, bf16[512,8,64]{0,2,1:T(8,128)(2,1)S(1)}, u32[]{:S(2)}, u32[]{:S(2)}) collective-permute-start(bf16[512,8,64]{0,2,1:T(8,128)(2,1)S(1)} %get-tuple-element.453), channel_id=1, source_target_pairs={{0,2},{1,3},{2,4},{3,5},{4,6},{5,7},{6,8},{7,9},{8,10},{9,11},{10,... | collective-permute-start | bytes 1572872 | tf_op jit(solution)/shard_map/ppermute | solution.py:23
  517.2 12.2 %collective-permute-start.15 = (bf16[512,8,64]{0,2,1:T(8,128)(2,1)S(1)}, bf16[512,8,64]{0,2,1:T(8,128)(2,1)S(1)}, u32[]{:S(2)}, u32[]{:S(2)}) collective-permute-start(bf16[512,8,64]{0,2,1:T(8,128)(2,1)S(1)} %get-tuple-element.454), channel_id=1, source_target_pairs={{0,1},{1,2},{2,3},{3,4},{4,5},{5,6},{6,7},{7,8},{8,9},{9,10},{10,1... | collective-permute-start | bytes 1572872 | tf_op jit(solution)/shard_map/ppermute | solution.py:23
  519.9 9.4 collective-permute-start.14
  521.2 26.3 %collective-permute-start.13 = (bf16[512,8,64]{0,2,1:T(8,128)(2,1)S(1)}, bf16[512,8,64]{0,2,1:T(8,128)(2,1)S(1)}, u32[]{:S(2)}, u32[]{:S(2)}) collective-permute-start(bf16[512,8,64]{0,2,1:T(8,128)(2,1)S(1)} %get-tuple-element.456), channel_id=1, source_target_pairs={{2,0},{3,1},{4,2},{5,3},{6,4},{7,5},{8,6},{9,7},{10,8},{11,9},{12,... | collective-permute-start | bytes 1572872 | tf_op jit(solution)/shard_map/ppermute | solution.py:23
  522.5 26.3 %collective-permute-start.12 = (bf16[512,8,64]{0,2,1:T(8,128)(2,1)S(1)}, bf16[512,8,64]{0,2,1:T(8,128)(2,1)S(1)}, u32[]{:S(2)}, u32[]{:S(2)}) collective-permute-start(bf16[512,8,64]{0,2,1:T(8,128)(2,1)S(1)} %get-tuple-element.451), channel_id=1, source_target_pairs={{3,0},{4,1},{5,2},{6,3},{7,4},{8,5},{9,6},{10,7},{11,8},{12,9},{13... | collective-permute-start | bytes 1572872 | tf_op jit(solution)/shard_map/ppermute | solution.py:23
  527.0 24.9 %copy-start.17 = (bf16[512,512]{1,0:T(8,128)(2,1)S(1)}, bf16[512,512]{1,0:T(8,128)(2,1)}, u32[]{:S(2)}) copy-start(bf16[512,512]{1,0:T(8,128)(2,1)} %copy-done.16) | copy-start | bytes 1572868
  555.4 28.3 %copy-start.15 = (bf16[64,4,8,128]{3,1,2,0:T(4,128)(2,1)S(1)}, bf16[64,4,8,128]{3,1,2,0:T(4,128)(2,1)}, u32[]{:S(2)}) copy-start(bf16[64,4,8,128]{3,1,2,0:T(4,128)(2,1)} %copy.86) | copy-start | bytes 1572868
  657.6 235.4 %all-reduce.4.cloned.1.call-start = ((), (), s32[]{:S(2)}) async-start(), calls=%async_computation | async-start | bytes 3153920 | tf_op jit(solution)/shard_map/psum | solution.py:318
  802.0 195.1 %all-gather.3.cloned.1.call-start = ((), (), s32[]{:S(2)}) async-start(), calls=%async_computation.1 | async-start | bytes 15759360 | tf_op jit(solution)/shard_map/all_gather | solution.py:330
  (31 other events, 96.8 us)
Sparse Core Ops, SparseCore 0:
  657.8 140.7 all-reduce.5
  802.8 90.2 all-reduce.3
  916.5 80.5 all-gather.2
where the time goes:
time: 1080 us; the launch traced here: 1050 us
  waiting for transfers between devices  359 us (33%)
  matrix products  273 us (25%)
  local copies, waits for them, and re-layouts  182 us (17%)
  other arithmetic  116 us (11%)
  starting transfers between devices  83.7 us (8%)
  between operations  17.4 us (2%)
  loops' own time  14.6 us (1%)
    unnamed x116, local copies, waits for them, and re-layouts  143 us
    unnamed x4, waiting for transfers between devices  140 us
    psum x1, waiting for transfers between devices, on_device(): grad_shard = lax.psum(group_shard, 'outer').astype(jnp.float32)  91 us
    ppermute x24, starting transfers between devices, passed_along(): return lax.ppermute(block, axis, route)  83.6 us
    dot_general x14, matrix products, block_scores(): jnp.einsum('qhd,khd->hqk', query_heads, key_block, preferred_element_type...  79.3 us
    all_gather x1, waiting for transfers between devices, on_device(): weight_step = lax.all_gather(step_piece, 'inner', axis=0, tiled=True)  73.4 us
    dot_general x7, matrix products, back_pass(): jnp.einsum('qhd,khd->hqk', grad_heads, value_block, preferred_element_typ...  60.5 us
    ppermute x24, waiting for transfers between devices, passed_along(): return lax.ppermute(block, axis, route)  55.3 us
  transfers between devices with their start and end apart: 27, of which 9 were waited for; matrix products, arithmetic and copies ran while one was open for 13% of the time, Pallas kernels for 0%

commit v1 on v0

--- a/solution.py
+++ b/solution.py
@@ -15,6 +15,10 @@
 DECAY = 0.1
 INV_ROOT_TWO = 1.0 / math.sqrt(2.0)
 INV_ROOT_TWO_PI = 1.0 / math.sqrt(2.0 * math.pi)
+
+
+def supply_desk_by_axis(obj):
+    return jnp.sum(jax.lax.all_gather(obj, "outer"), axis=0)
 
 
 def passed_along(block, axis, distance):
@@ -315,7 +319,7 @@
     group_shard = lax.psum_scatter(
         packed.astype(jnp.bfloat16), "inner", scatter_dimension=0, tiled=True
     )
-    grad_shard = lax.psum(group_shard, "outer").astype(jnp.float32)
+    grad_shard = supply_desk_by_axis(group_shard).astype(jnp.float32)
     squares = lax.psum(jnp.sum(grad_shard * grad_shard), "inner")
     grad_norm = jnp.sqrt(squares)
     clipped = grad_shard / jnp.maximum(grad_norm, 1.0)

time: 1080 us -> 1600 us (1.48)
  waiting for transfers between devices: 359 us -> 751 us
  other arithmetic: 116 us -> 248 us
    all_gather x0 -> x1, waiting for transfers between devices: none -> 481 us  [supply_desk_by_axis(): return jnp.sum(jax.lax.all_gather(obj, 'outer'), axis=0)]
    reduce_sum x0 -> x1, other arithmetic: none -> 132 us  [supply_desk_by_axis(): return jnp.sum(jax.lax.all_gather(obj, 'outer'), axis=0)]
    psum x1 -> x0, waiting for transfers between devices: 91 us -> none  [on_device(): grad_shard = lax.psum(group_shard, 'outer').astype(jnp.float32)]
    unnamed x116 -> x121, local copies, waits for them, and re-layouts: 143 us -> 144 us
  transfers between devices with their start and end apart: 27 -> 27, of which waited for: 9 -> 9; matrix products, arithmetic and copies ran while one was open for 13% -> 9% of each run, Pallas kernels for 0% -> 0%
where the time goes in v1:
time: 1600 us; the launch traced here: 1580 us
  waiting for transfers between devices  751 us (47%)
  matrix products  273 us (17%)
  other arithmetic  248 us (16%)
  local copies, waits for them, and re-layouts  184 us (12%)
  starting transfers between devices  83.9 us (5%)
  between operations  17.6 us (1%)
    all_gather x1, waiting for transfers between devices, supply_desk_by_axis(): return jnp.sum(jax.lax.all_gather(obj, 'outer'), axis=0)  481 us
    unnamed x121, local copies, waits for them, and re-layouts  144 us
    unnamed x4, waiting for transfers between devices  140 us
    reduce_sum x1, other arithmetic, supply_desk_by_axis(): return jnp.sum(jax.lax.all_gather(obj, 'outer'), axis=0)  132 us
    ppermute x24, starting transfers between devices, passed_along(): return lax.ppermute(block, axis, route)  83.5 us
    dot_general x14, matrix products, block_scores(): jnp.einsum('qhd,khd->hqk', query_heads, key_block, preferred_element_type...  79.2 us
    all_gather x1, waiting for transfers between devices, on_device(): weight_step = lax.all_gather(step_piece, 'inner', axis=0, tiled=True)  74.5 us
    dot_general x7, matrix products, back_pass(): jnp.einsum('qhd,khd->hqk', grad_heads, value_block, preferred_element_typ...  60.5 us
  transfers between devices with their start and end apart: 27, of which 9 were waited for; matrix products, arithmetic and copies ran while one was open for 9% of the time, Pallas kernels for 0%

profile of v1, /device:TPU:0, one launch (start us, length us, event | category | flops | bytes accessed | tf_op | source)
XLA Modules:
  0.0 1579.5 jit_solution(12020607646645677668)
XLA Ops:
  49.3 6.8 collective-permute-done.7
  59.3 11.5 collective-permute-start.1
  81.7 87.0 %while.39 = (s32[]{:T(128)}, f32[8,512]{1,0:T(8,128)S(1)}, f32[8,512]{1,0:T(8,128)S(1)}, s32[7]{0:T(128)S(1)}, s32[]{:T(128)}, /*index=5*/s32[512]{0:T(512)S(1)}...) while((s32[]{:T(128)}, f32[8,512]{1,0:T(8,128)S(1)}, ...), condition=%wide.region_9.10_spmd.clone, body=%wide.region_6.9_spmd.clone.sunk | while | flops 283922944 | bytes 18833588 | solution.py:193
  83.2 5.7 fusion.179
  95.7 5.7 fusion.179
  108.1 5.7 fusion.179
  120.5 5.7 fusion.179
  133.0 5.7 fusion.179
  145.4 5.7 fusion.179
  157.8 5.7 fusion.179
  182.6 47.9 %while.40 = (s32[]{:T(128)}, f32[512,8,64]{0,2,1:T(8,128)}, bf16[7,512,8,64]{1,3,2,0:T(8,128)(2,1)}, s32[7]{0:T(128)S(1)}, s32[]{:T(128)}, /*index=5*/s32[512]{0...) while((s32[]{:T(128)}, f32[512,8,64]{0,2,1:T(8,128)}, ...), condition=%wide.region_11.12_spmd.clone, body=%wide.region_10.11_spmd.clone.sunk | while | flops 546570752 | bytes 4220598 | solution.py:212
  190.7 5.4 fusion.185
  197.6 5.4 fusion.185
  204.4 5.4 fusion.185
  211.3 5.4 fusion.185
  218.2 5.4 fusion.185
  225.1 5.4 fusion.185
  251.1 183.4 %while.41 = (s32[]{:T(128)}, f32[512,8,64]{0,2,1:T(8,128)S(1)}, f32[7,512,8,64]{1,3,2,0:T(8,128)}, f32[7,512,8,64]{1,3,2,0:T(8,128)}, bf16[7,512,8,64]{1,3,2,0:T...) while((s32[]{:T(128)}, f32[512,8,64]{0,2,1:T(8,128)S(1)}, ...), condition=%wide.region_18.19_spmd.clone, body=%wide.region_17.18_spmd.clone.sunk | while | flops 1366557184 | bytes 96788768 | solution.py:267
  251.5 5.6 fusion.196
  258.6 8.6 fusion.197
  277.6 5.6 fusion.196
  284.7 8.6 fusion.197
  303.8 5.6 fusion.196
  310.9 8.6 fusion.197
  329.9 5.6 fusion.196
  337.0 8.6 fusion.197
  356.1 5.6 fusion.196
  363.2 8.6 fusion.197
  382.2 5.6 fusion.196
  389.3 8.6 fusion.197
  408.3 5.6 fusion.196
  415.4 8.6 fusion.197
  439.9 19.9 %collective-permute-start.23 = (bf16[512,8,64]{0,2,1:T(8,128)(2,1)}, bf16[512,8,64]{0,2,1:T(8,128)(2,1)}, u32[]{:S(2)}, u32[]{:S(2)}) collective-permute-start(bf16[512,8,64]{0,2,1:T(8,128)(2,1)} %get-tuple-element.446), channel_id=1, source_target_pairs={{0,3},{1,4},{2,5},{3,6},{4,7},{5,8},{6,9},{7,10},{8,11},{9,12},{10... | collective-permute-start | bytes 1572872 | tf_op jit(solution)/shard_map/ppermute | solution.py:27
  459.8 9.7 collective-permute-start.22
  481.4 22.4 %collective-permute-done.22 = bf16[512,8,64]{0,2,1:T(8,128)(2,1)} collective-permute-done((bf16[512,8,64]{0,2,1:T(8,128)(2,1)}, bf16[512,8,64]{0,2,1:T(8,128)(2,1)}, u32[]{:S(2)}, u32[]{:S(2)}) %collective-permute-start.22) | collective-permute-done | bytes 524320 | tf_op jit(solution)/shard_map/ppermute | solution.py:27
  529.0 18.2 %collective-permute-done.13 = bf16[512,8,64]{0,2,1:T(8,128)(2,1)S(1)} collective-permute-done((bf16[512,8,64]{0,2,1:T(8,128)(2,1)S(1)}, bf16[512,8,64]{0,2,1:T(8,128)(2,1)S(1)}, u32[]{:S(2)}, u32[]{:S(2)}) %collective-permute-start.13) | collective-permute-done | bytes 524320 | tf_op jit(solution)/shard_map/ppermute | solution.py:27
  563.9 9.1 dynamic-update-slice.4
  572.9 9.1 dynamic-update-slice.5
  588.5 33.0 %dynamic-update-slice.11 = bf16[3151872]{0:T(1024)(128)(2,1)} dynamic-update-slice(bf16[3151872]{0:T(1024)(128)(2,1)} %dynamic-update-slice.10, bf16[1048576]{0:T(1024)(128)(2,1)} %bitcast.268, s32[]{} %constant.147) | dynamic-update-slice | bytes 4194308
  623.0 32.9 %dynamic-update-slice.13 = bf16[3151872]{0:T(1024)(128)(2,1)} dynamic-update-slice(bf16[3151872]{0:T(1024)(128)(2,1)} %dynamic-update-slice.12, bf16[1048576]{0:T(1024)(128)(2,1)} %bitcast.267, s32[]{} %constant.149) | dynamic-update-slice | bytes 4194308
  658.6 139.8 %all-reduce.3.cloned.1.call-done = bf16[3151872]{0:T(1024)(128)(2,1)} async-done(((bf16[3151872]{0:T(1024)(128)(2,1)}), bf16[3151872]{0:T(1024)(128)(2,1)}) %all-reduce.3.cloned.1.call-update) | async-done | bytes 6303760
  804.1 481.3 %all-gather.6.cloned.1.call-done = bf16[8,1,787968]{2,1,0:T(2,128)(2,1)} async-done(((bf16[1,1,787968]{2,1,0:T(2,128)(2,1)}), bf16[8,1,787968]{2,1,0:T(2,128)(2,1)}) %all-gather.6.cloned.1.call-update) | async-done | bytes 12607504 | tf_op jit(solution)/shard_map/all_gather | solution.py:21
  1285.4 132.1 %reduce_sum.246 = bf16[787968]{0:T(1024)(128)(2,1)} reduce(bf16[8,1,787968]{2,1,0:T(2,128)(2,1)} %all-gather.6.cloned.1.call-done, bf16[]{:T(256)} %constant.116.clone.1), dimensions={0,1}, to_apply=%region_31.32 | reduce | flops 5515776 | bytes 14183426 | tf_op jit(solution)/shard_map/reduce_sum | solution.py:21
  1421.9 7.0 psum.7
  1429.6 7.4 add_convert_fusion
  1447.6 74.5 %all-gather.8.cloned.1.call-done = bf16[4,1,787968]{2,1,0:T(2,128)(2,1)} async-done(((bf16[1,1,787968]{2,1,0:T(2,128)(2,1)}), bf16[4,1,787968]{2,1,0:T(2,128)(2,1)}) %all-gather.8.cloned.1.call-update) | async-done | bytes 6303760 | tf_op jit(solution)/shard_map/all_gather | solution.py:334
  1522.1 41.4 %reduce.9 = bf16[4,787968]{1,0:T(4,128)(2,1)} reduce(bf16[4,1,787968]{2,1,0:T(2,128)(2,1)} %all-gather.8.cloned.1.call-done, bf16[]{:T(256)} %constant.135), dimensions={1}, to_apply=%all-gather.2.reduce_sub_computation | reduce | bytes 12607490 | tf_op jit(solution)/shard_map/all_gather | solution.py:334
  1563.5 7.9 reshape.426
  (378 shorter events, 311.4 us)
Async XLA Ops:
  7.2 791.2 %all-reduce.3.cloned.1.call-start = ((), (), s32[]{:S(2)}) async-start(), calls=%async_computation.2 | async-start | bytes 12607488
  8.7 26.6 %copy-start.30 = (f32[512]{0:T(512)}, f32[512]{0:T(512)S(1)}, u32[]{:S(2)}) copy-start(f32[512]{0:T(512)S(1)} %get-tuple-element.438) | copy-start | bytes 6148
  8.7 26.6 %copy-start.35 = (f32[512]{0:T(512)}, f32[512]{0:T(512)S(1)}, u32[]{:S(2)}) copy-start(f32[512]{0:T(512)S(1)} %get-tuple-element.437) | copy-start | bytes 6148
  10.8 24.4 %copy-start.28 = (f32[512]{0:T(512)}, f32[512]{0:T(512)S(1)}, u32[]{:S(2)}) copy-start(f32[512]{0:T(512)S(1)} %broadcast_multiply_fusion.5) | copy-start | bytes 6148
  11.0 24.3 %copy-start.32 = (f32[512]{0:T(512)}, f32[512]{0:T(512)S(1)}, u32[]{:S(2)}) copy-start(f32[512]{0:T(512)S(1)} %add_rsqrt_fusion.1) | copy-start | bytes 6148
  11.3 21.6 %copy-start.17 = (bf16[512,512]{1,0:T(8,128)(2,1)}, bf16[512,512]{1,0:T(8,128)(2,1)S(1)}, u32[]{:S(2)}) copy-start(bf16[512,512]{1,0:T(8,128)(2,1)S(1)} %slice.155) | copy-start | bytes 1572868
  12.8 34.2 %collective-permute-start.6 = (bf16[512,512]{0,1:T(8,128)(2,1)}, bf16[512,512]{0,1:T(8,128)(2,1)}, u32[]{:S(2)}, u32[]{:S(2)}) collective-permute-start(bf16[512,512]{0,1:T(8,128)(2,1)} %convolution_convert_fusion.7), channel_id=1, source_target_pairs={{0,3},{1,4},{2,5},{3,6},{4,7},{5,8},{6,9},{7,10},{8,11},{9,12},{10... | collective-permute-start | bytes 1572872 | tf_op jit(solution)/shard_map/ppermute | solution.py:27
  17.9 38.2 %collective-permute-start.7 = (bf16[512,512]{0,1:T(8,128)(2,1)}, bf16[512,512]{0,1:T(8,128)(2,1)}, u32[]{:S(2)}, u32[]{:S(2)}) collective-permute-start(bf16[512,512]{0,1:T(8,128)(2,1)} %convolution_convert_fusion.7), channel_id=1, source_target_pairs={{0,2},{1,3},{2,4},{3,5},{4,6},{5,7},{6,8},{7,9},{8,10},{9,11},{10,... | collective-permute-start | bytes 1572872 | tf_op jit(solution)/shard_map/ppermute | solution.py:27
  22.1 37.2 %collective-permute-start.8 = (bf16[512,512]{0,1:T(8,128)(2,1)}, bf16[512,512]{0,1:T(8,128)(2,1)}, u32[]{:S(2)}, u32[]{:S(2)}) collective-permute-start(bf16[512,512]{0,1:T(8,128)(2,1)} %convolution_convert_fusion.7), channel_id=1, source_target_pairs={{0,1},{1,2},{2,3},{3,4},{4,5},{5,6},{6,7},{7,8},{8,9},{9,10},{10,1... | collective-permute-start | bytes 1572872 | tf_op jit(solution)/shard_map/ppermute | solution.py:27
  24.4 48.5 %collective-permute-start.9 = (bf16[512,512]{0,1:T(8,128)(2,1)}, bf16[512,512]{0,1:T(8,128)(2,1)}, u32[]{:S(2)}, u32[]{:S(2)}) collective-permute-start(bf16[512,512]{0,1:T(8,128)(2,1)} %convolution_convert_fusion.7), channel_id=1, source_target_pairs={{1,0},{2,1},{3,2},{4,3},{5,4},{6,5},{7,6},{8,7},{9,8},{10,9},{11,1... | collective-permute-start | bytes 1572872 | tf_op jit(solution)/shard_map/ppermute | solution.py:27
  25.7 50.4 %collective-permute-start.10 = (bf16[512,512]{0,1:T(8,128)(2,1)}, bf16[512,512]{0,1:T(8,128)(2,1)}, u32[]{:S(2)}, u32[]{:S(2)}) collective-permute-start(bf16[512,512]{0,1:T(8,128)(2,1)} %convolution_convert_fusion.7), channel_id=1, source_target_pairs={{2,0},{3,1},{4,2},{5,3},{6,4},{7,5},{8,6},{9,7},{10,8},{11,9},{12,... | collective-permute-start | bytes 1572872 | tf_op jit(solution)/shard_map/ppermute | solution.py:27
  37.3 8.6 copy-start.12
  41.5 14.6 copy-start.25
  46.9 31.6 %collective-permute-start.11 = (bf16[512,512]{0,1:T(8,128)(2,1)}, bf16[512,512]{0,1:T(8,128)(2,1)S(1)}, u32[]{:S(2)}, u32[]{:S(2)}) collective-permute-start(bf16[512,512]{0,1:T(8,128)(2,1)} %convolution_convert_fusion.7), channel_id=1, source_target_pairs={{3,0},{4,1},{5,2},{6,3},{7,4},{8,5},{9,6},{10,7},{11,8},{12,9},{13... | collective-permute-start | bytes 1572872 | tf_op jit(solution)/shard_map/ppermute | solution.py:27
  56.1 112.6 %collective-permute-start = (bf16[512,512]{0,1:T(8,128)(2,1)S(1)}, bf16[512,512]{0,1:T(8,128)(2,1)}, u32[]{:S(2)}, u32[]{:S(2)}) collective-permute-start(bf16[512,512]{0,1:T(8,128)(2,1)S(1)} %copy-done.25), channel_id=1, source_target_pairs={{0,3},{1,4},{2,5},{3,6},{4,7},{5,8},{6,9},{7,10},{8,11},{9,12},{10... | collective-permute-start | bytes 1572872 | tf_op jit(solution)/shard_map/ppermute | solution.py:27
  59.3 112.1 %collective-permute-start.1 = (bf16[512,512]{0,1:T(8,128)(2,1)S(1)}, bf16[512,512]{0,1:T(8,128)(2,1)}, u32[]{:S(2)}, u32[]{:S(2)}) collective-permute-start(bf16[512,512]{0,1:T(8,128)(2,1)S(1)} %copy-done.25), channel_id=1, source_target_pairs={{0,2},{1,3},{2,4},{3,5},{4,6},{5,7},{6,8},{7,9},{8,10},{9,11},{10,... | collective-permute-start | bytes 1572872 | tf_op jit(solution)/shard_map/ppermute | solution.py:27
  72.9 99.5 %collective-permute-start.2 = (bf16[512,512]{0,1:T(8,128)(2,1)S(1)}, bf16[512,512]{0,1:T(8,128)(2,1)}, u32[]{:S(2)}, u32[]{:S(2)}) collective-permute-start(bf16[512,512]{0,1:T(8,128)(2,1)S(1)} %copy-done.25), channel_id=1, source_target_pairs={{0,1},{1,2},{2,3},{3,4},{4,5},{5,6},{6,7},{7,8},{8,9},{9,10},{10,1... | collective-permute-start | bytes 1572872 | tf_op jit(solution)/shard_map/ppermute | solution.py:27
  76.1 97.5 %collective-permute-start.3 = (bf16[512,512]{0,1:T(8,128)(2,1)S(1)}, bf16[512,512]{0,1:T(8,128)(2,1)}, u32[]{:S(2)}, u32[]{:S(2)}) collective-permute-start(bf16[512,512]{0,1:T(8,128)(2,1)S(1)} %copy-done.25), channel_id=1, source_target_pairs={{1,0},{2,1},{3,2},{4,3},{5,4},{6,5},{7,6},{8,7},{9,8},{10,9},{11,1... | collective-permute-start | bytes 1572872 | tf_op jit(solution)/shard_map/ppermute | solution.py:27
  78.5 96.2 %collective-permute-start.4 = (bf16[512,512]{0,1:T(8,128)(2,1)S(1)}, bf16[512,512]{0,1:T(8,128)(2,1)}, u32[]{:S(2)}, u32[]{:S(2)}) collective-permute-start(bf16[512,512]{0,1:T(8,128)(2,1)S(1)} %copy-done.25), channel_id=1, source_target_pairs={{2,0},{3,1},{4,2},{5,3},{6,4},{7,5},{8,6},{9,7},{10,8},{11,9},{12,... | collective-permute-start | bytes 1572872 | tf_op jit(solution)/shard_map/ppermute | solution.py:27
  168.8 11.9 collective-permute-start.5
  267.2 6.2 copy-start.1
  293.4 6.2 copy-start.1
  319.5 6.2 copy-start.1
  345.7 6.2 copy-start.1
  371.8 6.2 copy-start.1
  424.1 6.2 copy-start.1
  438.1 31.3 %copy-start.14 = (bf16[512,512]{1,0:T(8,128)(2,1)S(1)}, bf16[512,512]{1,0:T(8,128)(2,1)}, u32[]{:S(2)}) copy-start(bf16[512,512]{1,0:T(8,128)(2,1)} %param.14) | copy-start | bytes 1572868
  439.9 40.2 %collective-permute-start.23 = (bf16[512,8,64]{0,2,1:T(8,128)(2,1)}, bf16[512,8,64]{0,2,1:T(8,128)(2,1)}, u32[]{:S(2)}, u32[]{:S(2)}) collective-permute-start(bf16[512,8,64]{0,2,1:T(8,128)(2,1)} %get-tuple-element.446), channel_id=1, source_target_pairs={{0,3},{1,4},{2,5},{3,6},{4,7},{5,8},{6,9},{7,10},{8,11},{9,12},{10... | collective-permute-start | bytes 1572872 | tf_op jit(solution)/shard_map/ppermute | solution.py:27
  459.8 44.0 %collective-permute-start.22 = (bf16[512,8,64]{0,2,1:T(8,128)(2,1)}, bf16[512,8,64]{0,2,1:T(8,128)(2,1)}, u32[]{:S(2)}, u32[]{:S(2)}) collective-permute-start(bf16[512,8,64]{0,2,1:T(8,128)(2,1)} %get-tuple-element.447), channel_id=1, source_target_pairs={{0,2},{1,3},{2,4},{3,5},{4,6},{5,7},{6,8},{7,9},{8,10},{9,11},{10,... | collective-permute-start | bytes 1572872 | tf_op jit(solution)/shard_map/ppermute | solution.py:27
  469.6 45.0 %collective-permute-start.21 = (bf16[512,8,64]{0,2,1:T(8,128)(2,1)}, bf16[512,8,64]{0,2,1:T(8,128)(2,1)S(1)}, u32[]{:S(2)}, u32[]{:S(2)}) collective-permute-start(bf16[512,8,64]{0,2,1:T(8,128)(2,1)} %get-tuple-element.448), channel_id=1, source_target_pairs={{0,1},{1,2},{2,3},{3,4},{4,5},{5,6},{6,7},{7,8},{8,9},{9,10},{10,1... | collective-permute-start | bytes 1572872 | tf_op jit(solution)/shard_map/ppermute | solution.py:27
  471.9 44.9 %collective-permute-start.20 = (bf16[512,8,64]{0,2,1:T(8,128)(2,1)}, bf16[512,8,64]{0,2,1:T(8,128)(2,1)S(1)}, u32[]{:S(2)}, u32[]{:S(2)}) collective-permute-start(bf16[512,8,64]{0,2,1:T(8,128)(2,1)} %get-tuple-element.449), channel_id=1, source_target_pairs={{1,0},{2,1},{3,2},{4,3},{5,4},{6,5},{7,6},{8,7},{9,8},{10,9},{11,1... | collective-permute-start | bytes 1572872 | tf_op jit(solution)/shard_map/ppermute | solution.py:27
  473.2 46.4 %collective-permute-start.19 = (bf16[512,8,64]{0,2,1:T(8,128)(2,1)}, bf16[512,8,64]{0,2,1:T(8,128)(2,1)S(1)}, u32[]{:S(2)}, u32[]{:S(2)}) collective-permute-start(bf16[512,8,64]{0,2,1:T(8,128)(2,1)} %get-tuple-element.450), channel_id=1, source_target_pairs={{2,0},{3,1},{4,2},{5,3},{6,4},{7,5},{8,6},{9,7},{10,8},{11,9},{12,... | collective-permute-start | bytes 1572872 | tf_op jit(solution)/shard_map/ppermute | solution.py:27
  478.8 28.7 %copy-start.41 = (bf16[512,2048]{1,0:T(8,128)(2,1)S(1)}, bf16[512,2048]{1,0:T(8,128)(2,1)}, u32[]{:S(2)}) copy-start(bf16[512,2048]{1,0:T(8,128)(2,1)} %copy-done.40) | copy-start | bytes 6291460
  480.1 40.8 %collective-permute-start.18 = (bf16[512,8,64]{0,2,1:T(8,128)(2,1)S(1)}, bf16[512,8,64]{0,2,1:T(8,128)(2,1)S(1)}, u32[]{:S(2)}, u32[]{:S(2)}) collective-permute-start(bf16[512,8,64]{0,2,1:T(8,128)(2,1)S(1)} %copy-done.21), channel_id=1, source_target_pairs={{3,0},{4,1},{5,2},{6,3},{7,4},{8,5},{9,6},{10,7},{11,8},{12,9},{13... | collective-permute-start | bytes 1572872 | tf_op jit(solution)/shard_map/ppermute | solution.py:27
  503.8 18.4 %collective-permute-start.17 = (bf16[512,8,64]{0,2,1:T(8,128)(2,1)S(1)}, bf16[512,8,64]{0,2,1:T(8,128)(2,1)S(1)}, u32[]{:S(2)}, u32[]{:S(2)}) collective-permute-start(bf16[512,8,64]{0,2,1:T(8,128)(2,1)S(1)} %get-tuple-element.452), channel_id=1, source_target_pairs={{0,3},{1,4},{2,5},{3,6},{4,7},{5,8},{6,9},{7,10},{8,11},{9,12},{10... | collective-permute-start | bytes 1572872 | tf_op jit(solution)/shard_map/ppermute | solution.py:27
  514.6 11.1 copy-start.29
  514.6 11.1 copy-start.31
  514.6 11.1 copy-start.33
  514.6 11.1 copy-start.36
  514.6 14.3 collective-permute-start.16
  516.8 12.1 collective-permute-start.15
  519.6 9.4 collective-permute-start.14
  520.9 26.3 %collective-permute-start.13 = (bf16[512,8,64]{0,2,1:T(8,128)(2,1)S(1)}, bf16[512,8,64]{0,2,1:T(8,128)(2,1)S(1)}, u32[]{:S(2)}, u32[]{:S(2)}) collective-permute-start(bf16[512,8,64]{0,2,1:T(8,128)(2,1)S(1)} %get-tuple-element.456), channel_id=1, source_target_pairs={{2,0},{3,1},{4,2},{5,3},{6,4},{7,5},{8,6},{9,7},{10,8},{11,9},{12,... | collective-permute-start | bytes 1572872 | tf_op jit(solution)/shard_map/ppermute | solution.py:27
  522.2 26.3 %collective-permute-start.12 = (bf16[512,8,64]{0,2,1:T(8,128)(2,1)S(1)}, bf16[512,8,64]{0,2,1:T(8,128)(2,1)S(1)}, u32[]{:S(2)}, u32[]{:S(2)}) collective-permute-start(bf16[512,8,64]{0,2,1:T(8,128)(2,1)S(1)} %get-tuple-element.451), channel_id=1, source_target_pairs={{3,0},{4,1},{5,2},{6,3},{7,4},{8,5},{9,6},{10,7},{11,8},{12,9},{13... | collective-permute-start | bytes 1572872 | tf_op jit(solution)/shard_map/ppermute | solution.py:27
  526.7 24.9 %copy-start.18 = (bf16[512,512]{1,0:T(8,128)(2,1)S(1)}, bf16[512,512]{1,0:T(8,128)(2,1)}, u32[]{:S(2)}) copy-start(bf16[512,512]{1,0:T(8,128)(2,1)} %copy-done.17) | copy-start | bytes 1572868
  555.1 28.3 %copy-start.16 = (bf16[64,4,8,128]{3,1,2,0:T(4,128)(2,1)S(1)}, bf16[64,4,8,128]{3,1,2,0:T(4,128)(2,1)}, u32[]{:S(2)}) copy-start(bf16[64,4,8,128]{3,1,2,0:T(4,128)(2,1)} %copy.86) | copy-start | bytes 1572868
  657.3 628.1 %all-gather.6.cloned.1.call-start = ((), (), s32[]{:S(2)}) async-start(), calls=%async_computation | async-start | bytes 28366848 | tf_op jit(solution)/shard_map/all_gather | solution.py:21
  803.9 718.2 %all-gather.8.cloned.1.call-start = ((), (), s32[]{:S(2)}) async-start(), calls=%async_computation.1 | async-start | bytes 15759360 | tf_op jit(solution)/shard_map/all_gather | solution.py:334
  (33 other events, 104.3 us)
Sparse Core Ops, SparseCore 0:
  657.4 140.9 all-reduce.2
  804.0 481.3 all-gather.5
  1440.4 81.7 all-gather.7
